TPU v7x, 32 devices: a whole 2x2x4 slice. The times are simulated.
32 devices in a mesh: island: 2 (over x), fsdp: 16 (over z, y, core).
Axes of the slice: x: 2, y: 2, z: 4, core: 2. Of those that a mesh axis runs over, the one named last changes fastest.
Arguments:
- inputs: bfloat16 [4096, 4096], P(('island', 'fsdp')), may hold values from -6 to 6
- key_grad: bfloat16 [4096, 512], P(('island', 'fsdp')), may hold values from -6 to 6
- weight: float32 [4096, 512], P('fsdp'), may hold values from -6 to 6
- gain: float32 [4096], P('fsdp'), may hold values from 0.25 to 1.75
- momentum: float32 [4096, 512], P('fsdp'), may hold values from -3 to 3
- gain_momentum: float32 [4096], P('fsdp'), may hold values from -3 to 3
Outputs:
- keys: bfloat16 [4096, 512], P(('island', 'fsdp'))
- input_gradient: bfloat16 [4096, 4096], P(('island', 'fsdp'))
- new_weight: float32 [4096, 512], P('fsdp')
- new_momentum: float32 [4096, 512], P('fsdp')
- new_gain: float32 [4096], P('fsdp')
- new_gain_momentum: float32 [4096], P('fsdp')
All inputs are finite; a program needn't handle non-finite values.
Results may differ from a plain program's by a relative error of at most 0.009.
Values may be sent and summed in bfloat16 or wider, within the bound.
A program may use at most 64 MiB of HBM per device.

v0:
```python
import jax
import jax.numpy as jnp
from jax import lax
from jax.sharding import PartitionSpec as P

epsilon = 1e-05
inner_rate = 0.5
gain_rate = 0.02
beta_momentum = 0.9
outer_rate = 0.7


def nesterov(param, velocity, delta):
    fresh = beta_momentum * velocity + delta
    return (param - outer_rate * (delta + beta_momentum * fresh), fresh)


def shards(inputs, key_grad, weight, gain, momentum, gain_momentum):
    weight_b = weight.astype(jnp.bfloat16)
    gain_broadcast = gain.astype(jnp.bfloat16)
    full_weight, full_gain = (
        lax.all_gather(weight_b, "fsdp", axis=0, tiled=True),
        lax.all_gather(gain_broadcast, "fsdp", axis=0, tiled=True),
    )
    scale = full_weight.shape[0] ** (-0.5)
    gain_expanded = full_gain.astype(jnp.float32)
    expanded_rows = inputs.astype(jnp.float32)
    inverse_norm = lax.rsqrt(
        jnp.mean(expanded_rows * expanded_rows, axis=1, keepdims=True) + epsilon
    )
    centered_input = expanded_rows * inverse_norm
    normalized_rows = (centered_input * gain_expanded).astype(jnp.bfloat16)
    keys = (
        jnp.dot(normalized_rows, full_weight, preferred_element_type=jnp.float32) * scale
    ).astype(jnp.bfloat16)
    columns = lax.all_to_all(normalized_rows.T, "fsdp", split_axis=0, concat_axis=1, tiled=True)
    normalized_gradient = (
        lax.dot_general(
            key_grad, full_weight, (((1,), (1,)), ((), ())), preferred_element_type=jnp.float32
        )
        * scale
    )
    gain_portion = jnp.sum(normalized_gradient * centered_input, axis=0)
    centered_gradient = normalized_gradient * gain_expanded
    key_output = jnp.mean(centered_gradient * centered_input, axis=1, keepdims=True)
    input_gradient = (inverse_norm * (centered_gradient - centered_input * key_output)).astype(
        jnp.bfloat16
    )
    gain_gradient = lax.psum_scatter(gain_portion, "fsdp", scatter_dimension=0, tiled=True)
    weight_grad = (
        jnp.dot(
            columns,
            lax.all_gather(key_grad, "fsdp", axis=0, tiled=True),
            preferred_element_type=jnp.float32,
        )
        * scale
    )
    weight_delta = inner_rate * weight_grad
    gain_delta = gain_rate * gain_gradient
    islands = lax.axis_size("island")
    summed_w, summed_g = (
        lax.psum(weight_delta.astype(jnp.bfloat16), "island").astype(jnp.float32),
        lax.psum(gain_delta.astype(jnp.bfloat16), "island").astype(jnp.float32),
    )
    new_weight, new_momentum = nesterov(weight, momentum, summed_w / islands)
    new_gain, new_gain_momentum = nesterov(gain, gain_momentum, summed_g / islands)
    return (keys, input_gradient, new_weight, new_momentum, new_gain, new_gain_momentum)


def solution(mesh):
    in_specs = (
        P(("island", "fsdp"), None),
        P(("island", "fsdp"), None),
        P("fsdp", None),
        P("fsdp"),
        P("fsdp", None),
        P("fsdp"),
    )
    out_specs = (
        P(("island", "fsdp"), None),
        P(("island", "fsdp"), None),
        P("fsdp", None),
        P("fsdp", None),
        P("fsdp"),
        P("fsdp"),
    )
    return jax.shard_map(shards, mesh=mesh, in_specs=in_specs, out_specs=out_specs, check_vma=False)
```

profile of v0, /device:TPU:8, one launch (start us, length us, event | category | flops | bytes accessed | tf_op | source)
XLA Modules:
  0.0 186.4 jit_solution(4801344034884289757)
XLA Ops:
  7.2 0.0 copy-start.3
  7.2 0.0 copy-start
  7.2 0.0 copy-start.4
  7.2 0.0 all-gather.4.cloned.1.call-start
  7.2 1.9 %convert_element_type.37 = bf16[256,512]{1,0:T(8,128)(2,1)} convert(f32[256,512]{1,0:T(8,128)} %param.8) | non-fusion elementwise | flops 131072 | bytes 786432 | tf_op jit(solution)/shard_map/convert_element_type | solution.py:19
  9.1 0.0 all-gather.4.cloned.1.call-update
  9.1 0.0 all-gather.6.cloned.1.call-start
  9.2 0.7 all-gather.6.cloned.1.call-update
  9.9 1.5 fusion.10
  11.4 0.0 copy-done.4
  11.4 18.9 %all-gather = bf16[16,1,256]{2,1,0:T(2,128)(2,1)S(1)} all-gather(bf16[1,1,256]{2,1,0:T(2,128)(2,1)S(1)} %reshape.28), channel_id=1, replica_groups=mesh['island'=2,'fsdp'=16] {'fsdp'}, dimensions={0}, use_global_device_ids=true | all-gather | bytes 8704 | tf_op jit(solution)/shard_map/all_gather | solution.py:23
  30.3 32.2 %all-gather.4.cloned.1.call-done = bf16[4096,512]{1,0:T(8,128)(2,1)} async-done(((bf16[256,512]{1,0:T(8,128)(2,1)}), bf16[4096,512]{1,0:T(8,128)(2,1)}) %all-gather.4.cloned.1.call-update) | async-done | bytes 4194320 | tf_op jit(solution)/shard_map/all_gather | solution.py:22
  62.5 3.9 %fusion.9 = (f32[4096]{0:T(1024)S(1)}, f32[128]{0:T(128)S(1)}, f32[128,4096]{1,0:T(8,128)S(1)}) fusion(bf16[128,4096]{1,0:T(8,128)(2,1)S(1)} %copy-done, f32[128]{0:T(128)S(1)} %add_rsqrt_fusion, f32[4096]{0:T(1024)S(1)} %broadcast_multiply_fusion, bf16[128,512]{1,0:T(8,128)(2,1)S(1)} %copy-done.3, bf16[4096,512]{1,0:T(8,128)(2,1)} %all-gather.4.cloned.1.call-done), kind=kOutput, calls=%fused_computation.11 | convolution fusion | flops 541060992 | bytes 7504896 | tf_op jit(solution)/shard_map/dot_general | solution.py:38
  66.4 1.7 fusion.8
  68.1 1.1 copy.16
  69.2 4.0 %all-to-all-start = ((bf16[16,256,128]{1,2,0:T(8,128)(2,1)}), bf16[16,256,128]{1,2,0:T(8,128)(2,1)S(1)}, u32[]{:S(2)}, u32[]{:S(2)}) async-start(bf16[16,256,128]{1,2,0:T(8,128)(2,1)} %bitcast.15), calls=%async_computation | async-start | bytes 2097152 | tf_op jit(solution)/shard_map/all_to_all | solution.py:36
  73.2 0.0 all-reduce.3.cloned.1.call-start
  73.2 0.0 copy-done.6
  73.2 0.6 dynamic-slice
  74.5 70.6 %all-reduce = f32[4096]{0:T(1024)S(1)} all-reduce(f32[4096]{0:T(1024)S(1)} %get-tuple-element.6), channel_id=2, replica_groups=mesh['island'=2,'fsdp'=16] {'fsdp'}, use_global_device_ids=true, to_apply=%region_4.0.clone | all-reduce | flops 4096 | bytes 32768
  145.1 3.6 %fusion.12 = bf16[128,512]{1,0:T(8,128)(2,1)} fusion(bf16[128,4096]{1,0:T(8,128)(2,1)S(1)} %get-tuple-element.13, bf16[4096,512]{1,0:T(8,128)(2,1)} %all-gather.4.cloned.1.call-done), kind=kOutput, calls=%fused_computation.16 | convolution fusion | flops 537001984 | bytes 5373952 | tf_op jit(solution)/shard_map/dot_general | solution.py:34
  148.7 0.0 all-to-all-done
  148.8 0.0 copy-start.2
  148.8 3.1 %fusion.11 = bf16[256,512]{1,0:T(8,128)(2,1)} fusion(bf16[256,2048]{0,1:T(8,128)(2,1)S(1)} %bitcast.17, bf16[2048,512]{1,0:T(8,128)(2,1)} %all-gather.6.cloned.1.call-done), kind=kOutput, calls=%fused_computation.14 | convolution fusion | flops 537133056 | bytes 3407872 | tf_op jit(solution)/shard_map/dot_general | solution.py:51
  151.9 0.0 all-reduce.3.cloned.1.call-update
  151.9 0.1 fusion.13
  152.0 4.9 %psum.15 = bf16[256]{0:T(256)(128)(2,1)S(1)} all-reduce(bf16[256]{0:T(256)(128)(2,1)S(1)} %fusion.13), channel_id=1, replica_groups=mesh['island'=2,'fsdp'=16] {'island'}, use_global_device_ids=true, to_apply=%region_5.0 | all-reduce | flops 256 | bytes 1024 | tf_op jit(solution)/shard_map/psum | solution.py:63
  156.9 0.0 copy-done.5
  156.9 0.6 multiply_subtract_fusion.1
  157.5 20.2 %all-reduce.3.cloned.1.call-done = bf16[256,512]{1,0:T(8,128)(2,1)} async-done(((bf16[256,512]{1,0:T(8,128)(2,1)}), bf16[256,512]{1,0:T(8,128)(2,1)}) %all-reduce.3.cloned.1.call-update) | async-done | bytes 262160 | tf_op jit(solution)/shard_map/psum | solution.py:62
  177.7 0.0 copy-done.2
  177.7 2.1 %multiply_subtract_fusion = (f32[256,512]{1,0:T(8,128)}, f32[256,512]{1,0:T(8,128)}) fusion(f32[256,512]{1,0:T(8,128)S(1)} %copy-done.1, bf16[256,512]{1,0:T(8,128)(2,1)} %all-reduce.3.cloned.1.call-done, f32[256,512]{1,0:T(8,128)S(1)} %copy-done.2), kind=kLoop, calls=%fused_computation.18 | loop fusion | flops 1048576 | bytes 2359296 | tf_op jit(solution)/shard_map/sub | solution.py:15
  (13 shorter events, 0.1 us)
Async XLA Ops:
  7.2 55.4 %copy-start.3 = (bf16[128,512]{1,0:T(8,128)(2,1)S(1)}, bf16[128,512]{1,0:T(8,128)(2,1)}, u32[]{:S(2)}) copy-start(bf16[128,512]{1,0:T(8,128)(2,1)} %param.7) | copy-start | bytes 393220
  7.2 55.4 %copy-start = (bf16[128,4096]{1,0:T(8,128)(2,1)S(1)}, bf16[128,4096]{1,0:T(8,128)(2,1)}, u32[]{:S(2)}) copy-start(bf16[128,4096]{1,0:T(8,128)(2,1)} %param.6) | copy-start | bytes 3145732
  7.2 4.2 %copy-start.4 = (f32[256]{0:T(256)S(1)}, f32[256]{0:T(256)}, u32[]{:S(2)}) copy-start(f32[256]{0:T(256)} %param.9) | copy-start | bytes 3076
  7.2 55.3 %all-gather.4.cloned.1.call-start = ((), (), s32[]{:S(2)}) async-start(), calls=%async_computation.1 | async-start | bytes 4456448 | tf_op jit(solution)/shard_map/all_gather | solution.py:22
  9.1 139.6 %all-gather.6.cloned.1.call-start = ((), (), s32[]{:S(2)}) async-start(), calls=%async_computation.2 | async-start | bytes 2228224 | tf_op jit(solution)/shard_map/all_gather | solution.py:53
  68.1 5.2 %copy-start.6 = (u32[32]{0:T(128)S(1)}, u32[32]{0:T(128)}, u32[]{:S(2)}) copy-start(u32[32]{0:T(128)} %constant.30) | copy-start | bytes 388
  69.2 79.6 %all-to-all-start = ((bf16[16,256,128]{1,2,0:T(8,128)(2,1)}), bf16[16,256,128]{1,2,0:T(8,128)(2,1)S(1)}, u32[]{:S(2)}, u32[]{:S(2)}) async-start(bf16[16,256,128]{1,2,0:T(8,128)(2,1)} %bitcast.15), calls=%async_computation | async-start | bytes 2097152 | tf_op jit(solution)/shard_map/all_to_all | solution.py:36
  73.2 104.5 %all-reduce.3.cloned.1.call-start = ((), (), s32[]{:S(2)}) async-start(), calls=%async_computation.3 | async-start | bytes 524288 | tf_op jit(solution)/shard_map/psum | solution.py:62
  148.7 8.2 %copy-start.5 = (f32[256]{0:T(256)S(1)}, f32[256]{0:T(256)}, u32[]{:S(2)}) copy-start(f32[256]{0:T(256)} %param.11) | copy-start | bytes 3076
  148.7 29.0 %copy-start.1 = (f32[256,512]{1,0:T(8,128)S(1)}, f32[256,512]{1,0:T(8,128)}, u32[]{:S(2)}) copy-start(f32[256,512]{1,0:T(8,128)} %param.8) | copy-start | bytes 1572868
  148.8 29.0 %copy-start.2 = (f32[256,512]{1,0:T(8,128)S(1)}, f32[256,512]{1,0:T(8,128)}, u32[]{:S(2)}) copy-start(f32[256,512]{1,0:T(8,128)} %param.10) | copy-start | bytes 1572868
Sparse Core Ops, SparseCore 0:
  10.8 51.7 all-gather.3
  64.7 45.8 all-gather.5
  152.0 25.6 all-reduce.2
where the time goes:
time: 188 us; the launch traced here: 186 us
  blocking collectives  94.4 us (50%)
  waiting for transfers between devices  53.2 us (28%)
  between operations  14.5 us (8%)
  matrix products  10.6 us (6%)
  other arithmetic  7.84 us (4%)
  starting transfers between devices  4.12 us (2%)
    unnamed x1, blocking collectives  70.6 us
    all_gather x1, waiting for transfers between devices, shards(): lax.all_gather(weight_b, 'fsdp', axis=0, tiled=True)  32.2 us
    psum x1, waiting for transfers between devices, shards(): lax.psum(weight_delta.astype(jnp.bfloat16), 'island').astype(jnp.float32)  20.2 us
    all_gather x1, blocking collectives, shards(): lax.all_gather(gain_broadcast, 'fsdp', axis=0, tiled=True)  18.9 us
    psum x1, blocking collectives, shards(): lax.psum(gain_delta.astype(jnp.bfloat16), 'island').astype(jnp.float32)  4.92 us
    all_to_all x1, starting transfers between devices, shards(): lax.all_to_all(normalized_rows.T, 'fsdp', split_axis=0, concat_axis=1, ti...  4 us
    dot_general x1, matrix products, shards(): lax.dot_general(key_grad, full_weight, (((1,), (1,)), ((), ())), preferre...  3.87 us
  transfers between devices with their start and end apart: 4, of which 2 were waited for; matrix products, arithmetic and copies ran while one was open for 7% of the time, Pallas kernels for 0%

commit v1 on v0

v1 whole, which is shorter than its diff:
```python
import functools

import jax
import jax.numpy as jnp
from jax import lax
from jax.experimental import pallas as pl
from jax.experimental.pallas import tpu as pltpu
from jax.sharding import PartitionSpec as P

epsilon = 1e-05
inner_rate = 0.5
gain_rate = 0.02
beta_momentum = 0.9
outer_rate = 0.7

MESH = pl.DeviceIdType.MESH
F32, BF16 = jnp.float32, jnp.bfloat16


def kernel(
    n_isl, a, b,
    x_ref, kg_ref, w_ref, g_ref, m_ref, gm_ref,
    keys_ref, ig_ref, nw_ref, nm_ref, ng_ref, ngm_ref,
    gw, xs, xr, kr, gs, gr, ge, dx, kacc,
    z_s, z_r, y_s, y_r, x_s, x_r, c_s, c_r, t_s, t_r, k_s, k_r, g_s, g_r, e_s, e_r,
):
    nq = 2 * b
    n = a * nq
    tokens, width = x_ref.shape
    rows, feats = w_ref.shape
    scale = width ** (-0.5)
    isl = lax.axis_index("island")
    f = lax.axis_index("fsdp")
    z, q = f // nq, f % nq
    y, core = q // 2, q % 2
    sib = y * 2 + 1 - core
    half = isl % 2
    partner = isl + 1 - 2 * half

    def dev(i, zz, qq):
        return (i, zz * nq + qq)

    def remote(src, dst, ss, rs, to):
        return pltpu.make_async_remote_copy(
            src_ref=src, dst_ref=dst, send_sem=ss, recv_sem=rs, device_id=to, device_id_type=MESH
        )

    zs_ = [lax.rem(z + k, a) for k in range(a)]
    qs_ = [lax.rem(q + k, nq) for k in range(nq)]
    ys_ = [lax.rem(y + k, b) for k in range(b)]
    is_ = [lax.rem(isl + k, n_isl) for k in range(n_isl)]

    barrier = pltpu.get_barrier_semaphore()
    for k in range(1, a):
        pl.semaphore_signal(barrier, inc=1, device_id=dev(isl, zs_[k], q), device_id_type=MESH)
    for k in range(1, nq):
        pl.semaphore_signal(barrier, inc=1, device_id=dev(isl, z, qs_[k]), device_id_type=MESH)
    for k in range(1, n_isl):
        pl.semaphore_signal(barrier, inc=1, device_id=dev(is_[k], z, q), device_id_type=MESH)

    lanes = min(rows, 128)
    gain_col = jnp.concatenate(
        [
            jnp.broadcast_to(
                g_ref[0:1, j * lanes : (j + 1) * lanes].astype(BF16).astype(F32), (lanes, lanes)
            ).T[:, 0:1]
            for j in range(rows // lanes)
        ],
        axis=0,
    )
    w_b = w_ref[...].astype(BF16).astype(F32)
    gw[z, q] = (w_b * gain_col).astype(BF16).reshape(2, rows // 2, feats)
    pl.semaphore_wait(barrier, a - 1 + nq - 1 + n_isl - 1)

    sends = []

    def go(copy):
        copy.start()
        sends.append(copy)

    def z_copy(k):
        p = gw.at[z, q, half]
        return remote(p, p, z_s.at[k], z_r.at[k], dev(isl, zs_[k], q))

    def z_wait(k):
        p = gw.at[lax.rem(z + a - k, a), q, half]
        remote(p, p, z_s.at[k], z_r.at[k], dev(isl, zs_[k], q)).wait_recv()

    def y_copy(zk, k):
        p = gw.at[lax.rem(z + a - zk, a), q, half]
        return remote(p, p, y_s.at[zk, k], y_r.at[zk, k], dev(isl, z, ys_[k] * 2 + core))

    def y_wait(zk, k):
        p = gw.at[lax.rem(z + a - zk, a), lax.rem(y + b - k, b) * 2 + core, half]
        remote(p, p, y_s.at[zk, k], y_r.at[zk, k], dev(isl, z, q)).wait_recv()

    def piece(zk, k):
        return lax.rem(z + a - zk, a), lax.rem(y + b - k, b) * 2 + core

    def x_copy(zk, k):
        zz, qq = piece(zk, k)
        p = gw.at[zz, qq, half]
        return remote(p, p, x_s.at[zk, k], x_r.at[zk, k], dev(partner, z, q))

    def x_wait(zk, k):
        zz, qq = piece(zk, k)
        p = gw.at[zz, qq, 1 - half]
        remote(p, p, x_s.at[zk, k], x_r.at[zk, k], dev(partner, z, q)).wait_recv()

    def c_copy(zk, k, h):
        zz, qq = piece(zk, k)
        p = gw.at[zz, qq, lax.rem(half + h, 2)]
        return remote(p, p, c_s.at[zk, k, h], c_r.at[zk, k, h], dev(isl, z, sib))

    def c_wait(zk, k, h):
        zz, qq = piece(zk, k)
        p = gw.at[zz, qq + 1 - 2 * core, lax.rem(half + h, 2)]
        remote(p, p, c_s.at[zk, k, h], c_r.at[zk, k, h], dev(isl, z, sib)).wait_recv()

    for k in range(1, a):
        go(z_copy(k))

    for k in range(1, nq):
        go(remote(kg_ref, kr.at[q], k_s.at[k], k_r.at[k], dev(isl, z, qs_[k])))

    acc = jnp.zeros((tokens, rows), F32)
    for p in range(n):
        xc = x_ref[:, p * rows : (p + 1) * rows].astype(F32)
        acc = acc + xc * xc
    r = lax.rsqrt(jnp.sum(acc, axis=1, keepdims=True) * (1.0 / width) + epsilon)
    for p in range(n):
        xc = x_ref[:, p * rows : (p + 1) * rows].astype(F32)
        xs[p % nq, p // nq] = (xc * r).astype(BF16)
    for k in range(1, nq):
        go(remote(xs.at[qs_[k]], xr.at[q], t_s.at[k], t_r.at[k], dev(isl, z, qs_[k])))
    xr[q] = xs[q]
    kr[q] = kg_ref[...]

    for k in range(1, b):
        go(y_copy(0, k))
    for h in range(2):
        go(c_copy(0, 0, h))

    for zk in range(1, a):
        z_wait(zk)
        for k in range(1, b):
            go(y_copy(zk, k))
        go(x_copy(zk, 0))
        go(c_copy(zk, 0, 0))

    for k in range(1, nq):
        src = lax.rem(q + nq - k, nq)
        remote(kg_ref, kr.at[src], k_s.at[k], k_r.at[k], dev(isl, z, q)).wait_recv()
        remote(xs.at[q], xr.at[src], t_s.at[k], t_r.at[k], dev(isl, z, q)).wait_recv()

    def partial(zz):
        return lax.dot_general(
            xr[:, zz].reshape(nq * tokens, rows),
            kr[...].reshape(nq * tokens, feats),
            (((0,), (0,)), ((), ())),
            preferred_element_type=F32,
        )

    for k in range(1, a):
        gs[k] = partial(zs_[k]).astype(BF16)
        go(remote(gs.at[k], gr.at[k], g_s.at[k], g_r.at[k], dev(isl, zs_[k], q)))
    own = partial(z)

    for zk in range(a):
        for k in range(1, b):
            y_wait(zk, k)
            go(x_copy(zk, k))
            go(c_copy(zk, k, 0))

    for k in range(1, a):
        remote(gs.at[k], gr.at[k], g_s.at[k], g_r.at[k], dev(isl, z, q)).wait_recv()
        own = own + gr[k].astype(F32)
    ge[isl] = own.astype(BF16)
    for k in range(1, n_isl):
        go(remote(ge.at[isl], ge.at[isl], e_s.at[k], e_r.at[k], dev(is_[k], z, q)))

    kacc[...] = jnp.zeros_like(kacc)

    def use(zz, qq):
        p = gw[zz, qq].reshape(rows, feats)
        kacc[...] += jnp.dot(xs[qq, zz], p, preferred_element_type=F32)
        dx[qq, zz] = lax.dot_general(
            kg_ref[...], p, (((1,), (1,)), ((), ())), preferred_element_type=F32
        )

    order = [(zk, k) for k in range(b) for zk in range(a)]
    for zk, k in order:
        if (zk, k) != (0, 0):
            x_wait(zk, k)
            go(c_copy(zk, k, 1))
        use(*piece(zk, k))
    for zk, k in order:
        c_wait(zk, k, 0)
        c_wait(zk, k, 1)
        zz, qq = piece(zk, k)
        use(zz, qq + 1 - 2 * core)

    keys_ref[...] = (kacc[...] * scale).astype(BF16)
    acc = jnp.zeros((tokens, rows), F32)
    for p in range(n):
        xh = x_ref[:, p * rows : (p + 1) * rows].astype(F32) * r
        acc = acc + dx[p % nq, p // nq] * xh
    mean = jnp.sum(acc, axis=1, keepdims=True) * (scale / width)
    for p in range(n):
        cols = slice(p * rows, (p + 1) * rows)
        xh = x_ref[:, cols].astype(F32) * r
        ig_ref[:, cols] = (r * (dx[p % nq, p // nq] * scale - xh * mean)).astype(BF16)

    for k in range(1, n_isl):
        src = lax.rem(isl + n_isl - k, n_isl)
        remote(ge.at[src], ge.at[src], e_s.at[k], e_r.at[k], dev(isl, z, q)).wait_recv()
    total = ge[0].astype(F32)
    for k in range(1, n_isl):
        total = total + ge[k].astype(F32)
    total = total * (scale / n_isl)
    delta = total * gain_col * inner_rate
    w = w_ref[...]
    fresh = beta_momentum * m_ref[...] + delta
    nm_ref[...] = fresh
    nw_ref[...] = w - outer_rate * (delta + beta_momentum * fresh)
    gain_sum = jnp.sum(w.astype(BF16).astype(F32) * total, axis=1, keepdims=True) * gain_rate
    for j in range(rows // lanes):
        s = slice(j * lanes, (j + 1) * lanes)
        d = jnp.broadcast_to(gain_sum[s], (lanes, lanes)).T[0:1]
        fresh = beta_momentum * gm_ref[0:1, s] + d
        ngm_ref[0:1, s] = fresh
        ng_ref[0:1, s] = g_ref[0:1, s] - outer_rate * (d + beta_momentum * fresh)

    for copy in sends:
        copy.wait_send()


def solution(mesh):
    n_isl, n = mesh.shape["island"], mesh.shape["fsdp"]
    b = 1
    while 4 * b * b <= n // 2:
        b *= 2
    a = n // 2 // b
    nq = 2 * b

    def shards(inputs, key_grad, weight, gain, momentum, gain_momentum):
        tokens, width = inputs.shape
        rows, feats = weight.shape
        sd = jax.ShapeDtypeStruct
        dma = pltpu.SemaphoreType.DMA
        vm = pl.BlockSpec(memory_space=pltpu.VMEM)
        outs = pl.pallas_call(
            functools.partial(kernel, n_isl, a, b),
            out_shape=(
                sd((tokens, feats), BF16),
                sd((tokens, width), BF16),
                sd((rows, feats), F32),
                sd((rows, feats), F32),
                sd((1, rows), F32),
                sd((1, rows), F32),
            ),
            in_specs=[vm] * 6,
            out_specs=[vm] * 6,
            scratch_shapes=[
                pltpu.VMEM((a, nq, 2, rows // 2, feats), BF16),
                pltpu.VMEM((nq, a, tokens, rows), BF16),
                pltpu.VMEM((nq, a, tokens, rows), BF16),
                pltpu.VMEM((nq, tokens, feats), BF16),
                pltpu.VMEM((a, rows, feats), BF16),
                pltpu.VMEM((a, rows, feats), BF16),
                pltpu.VMEM((n_isl, rows, feats), BF16),
                pltpu.VMEM((nq, a, tokens, rows), F32),
                pltpu.VMEM((tokens, feats), F32),
                dma((a,)), dma((a,)),
                dma((a, b)), dma((a, b)),
                dma((a, b)), dma((a, b)),
                dma((a, b, 2)), dma((a, b, 2)),
                dma((nq,)), dma((nq,)),
                dma((nq,)), dma((nq,)),
                dma((a,)), dma((a,)),
                dma((n_isl,)), dma((n_isl,)),
            ],
            compiler_params=pltpu.CompilerParams(
                collective_id=0, has_side_effects=True, vmem_limit_bytes=48 << 20
            ),
        )(inputs, key_grad, weight, gain.reshape(1, rows), momentum, gain_momentum.reshape(1, rows))
        keys, ig, nw, nm, ng, ngm = outs
        return keys, ig, nw, nm, ng.reshape(rows), ngm.reshape(rows)

    in_specs = (
        P(("island", "fsdp"), None),
        P(("island", "fsdp"), None),
        P("fsdp", None),
        P("fsdp"),
        P("fsdp", None),
        P("fsdp"),
    )
    out_specs = (
        P(("island", "fsdp"), None),
        P(("island", "fsdp"), None),
        P("fsdp", None),
        P("fsdp", None),
        P("fsdp"),
        P("fsdp"),
    )
    return jax.shard_map(shards, mesh=mesh, in_specs=in_specs, out_specs=out_specs, check_vma=False)
```

time: 188 us -> 61.4 us (0.33)
  blocking collectives: 94.4 us -> 0 us
  waiting for transfers between devices: 53.2 us -> 0 us
  Pallas kernels: 0 us -> 51.2 us
  between operations: 14.5 us -> 0.67 us
  matrix products: 10.6 us -> 0 us
  other arithmetic: 7.84 us -> 0 us
  local copies, waits for them, and re-layouts: 1.72 us -> 9.23 us
  starting transfers between devices: 4.12 us -> 0 us
    unnamed x1 -> x0, blocking collectives: 70.6 us -> none
    pallas_call x0 -> x1, Pallas kernels: none -> 51.2 us  [shards(): pl.pallas_call(functools.partial(kernel, n_isl, a, b), out_shape=(sd((tok...]
    all_gather x2 -> x0, waiting for transfers between devices: 32.2 us -> none  [the longest x1 32.2 us: shards(): lax.all_gather(weight_b, 'fsdp', axis=0, tiled=True)]
    psum x1 -> x0, waiting for transfers between devices: 20.2 us -> none  [shards(): lax.psum(weight_delta.astype(jnp.bfloat16), 'island').astype(jnp.float32)]
    all_gather x1 -> x0, blocking collectives: 18.9 us -> none  [shards(): lax.all_gather(gain_broadcast, 'fsdp', axis=0, tiled=True)]
    dot_general x3 -> x0, matrix products: 10.6 us -> none  [the longest x1 3.87 us: shards(): lax.dot_general(key_grad, full_weight, (((1,), (1,)), ((), ())), preferre...]
    unnamed x16 -> x18, local copies, waits for them, and re-layouts: 0.62 us -> 9.23 us
    psum x1 -> x0, blocking collectives: 4.92 us -> none  [shards(): lax.psum(gain_delta.astype(jnp.bfloat16), 'island').astype(jnp.float32)]
  transfers between devices with their start and end apart: 4 -> 0, of which waited for: 2 -> 0; matrix products, arithmetic and copies ran while one was open for 7% -> 0% of each run, Pallas kernels for 0% -> 0%
where the time goes in v1:
time: 61.4 us; the launch traced here: 61.1 us
  Pallas kernels  51.2 us (83%)
  local copies, waits for them, and re-layouts  9.23 us (15%)
  between operations  0.67 us (1%)
    pallas_call x1, Pallas kernels, shards(): pl.pallas_call(functools.partial(kernel, n_isl, a, b), out_shape=(sd((tok...  51.2 us
    unnamed x18, local copies, waits for them, and re-layouts  9.23 us

profile of v1, /device:TPU:8, one launch (start us, length us, event | category | flops | bytes accessed | tf_op | source)
XLA Modules:
  0.0 61.1 jit_solution(14837110843706087259)
XLA Ops:
  0.6 0.0 copy-start.5
  0.6 0.0 copy-start.4
  0.7 0.7 %copy-done.5 = f32[256]{0:T(256)S(1)} copy-done((f32[256]{0:T(256)S(1)}, f32[256]{0:T(256)}, u32[]{:S(2)}) %copy-start.5) | copy-done | bytes 1048
  1.3 0.0 copy-done.4
  1.3 0.0 copy-start
  1.3 1.2 %copy-done = bf16[128,4096]{1,0:T(8,128)(2,1)S(1)} copy-done((bf16[128,4096]{1,0:T(8,128)(2,1)S(1)}, bf16[128,4096]{1,0:T(8,128)(2,1)}, u32[]{:S(2)}) %copy-start) | copy-done | bytes 1048600
  2.6 0.0 copy-start.1
  2.6 1.0 %copy-done.1 = f32[256,512]{1,0:T(8,128)S(1)} copy-done((f32[256,512]{1,0:T(8,128)S(1)}, f32[256,512]{1,0:T(8,128)}, u32[]{:S(2)}) %copy-start.1) | copy-done | bytes 524312
  3.6 0.0 copy-start.2
  3.6 1.0 %copy-done.2 = f32[256,512]{1,0:T(8,128)S(1)} copy-done((f32[256,512]{1,0:T(8,128)S(1)}, f32[256,512]{1,0:T(8,128)}, u32[]{:S(2)}) %copy-start.2) | copy-done | bytes 524312
  4.6 0.0 copy-start.3
  4.6 0.9 %copy-done.3 = bf16[128,512]{1,0:T(8,128)(2,1)S(1)} copy-done((bf16[128,512]{1,0:T(8,128)(2,1)S(1)}, bf16[128,512]{1,0:T(8,128)(2,1)}, u32[]{:S(2)}) %copy-start.3) | copy-done | bytes 131096
  5.5 51.2 %shard_map.109 = (bf16[128,512]{1,0:T(8,128)(2,1)S(1)}, bf16[128,4096]{1,0:T(8,128)(2,1)S(1)}, f32[256,512]{1,0:T(8,128)S(1)}, f32[256,512]{1,0:T(8,128)S(1)}, f...) custom-call(bf16[128,4096]{1,0:T(8,128)(2,1)S(1)} %copy-done, bf16[128,512]{1,0:T(8,128)(2,1)S(1)} %copy-done.3, ...), custom_call_target="tpu_custom_call" | custom-call | tf_op jit(solution)/shard_map/pallas_call | solution.py:252
  56.7 0.7 %copy.18 = bf16[128,512]{1,0:T(8,128)(2,1)} copy(bf16[128,512]{1,0:T(8,128)(2,1)S(1)} %get-tuple-element.24) | data formatting | bytes 262144
  57.4 1.0 %copy.19 = bf16[128,4096]{1,0:T(8,128)(2,1)} copy(bf16[128,4096]{1,0:T(8,128)(2,1)S(1)} %get-tuple-element.25) | data formatting | bytes 2097152
  58.4 0.8 %copy.20 = f32[256,512]{1,0:T(8,128)} copy(f32[256,512]{1,0:T(8,128)S(1)} %get-tuple-element.26) | data formatting | bytes 1048576
  59.2 0.8 %copy.21 = f32[256,512]{1,0:T(8,128)} copy(f32[256,512]{1,0:T(8,128)S(1)} %get-tuple-element.27) | data formatting | bytes 1048576
  59.9 0.6 copy.22
  60.5 0.6 copy.23
Async XLA Ops:
  0.6 0.7 %copy-start.5 = (f32[256]{0:T(256)S(1)}, f32[256]{0:T(256)}, u32[]{:S(2)}) copy-start(f32[256]{0:T(256)} %param.11) | copy-start | bytes 3076
  0.6 0.7 %copy-start.4 = (f32[256]{0:T(256)S(1)}, f32[256]{0:T(256)}, u32[]{:S(2)}) copy-start(f32[256]{0:T(256)} %param.9) | copy-start | bytes 3076
  1.3 1.2 %copy-start = (bf16[128,4096]{1,0:T(8,128)(2,1)S(1)}, bf16[128,4096]{1,0:T(8,128)(2,1)}, u32[]{:S(2)}) copy-start(bf16[128,4096]{1,0:T(8,128)(2,1)} %x_ref.1) | copy-start | bytes 3145732
  2.6 1.0 %copy-start.1 = (f32[256,512]{1,0:T(8,128)S(1)}, f32[256,512]{1,0:T(8,128)}, u32[]{:S(2)}) copy-start(f32[256,512]{1,0:T(8,128)} %w_ref.1) | copy-start | bytes 1572868
  3.6 1.0 %copy-start.2 = (f32[256,512]{1,0:T(8,128)S(1)}, f32[256,512]{1,0:T(8,128)}, u32[]{:S(2)}) copy-start(f32[256,512]{1,0:T(8,128)} %m_ref.1) | copy-start | bytes 1572868
  4.6 0.9 %copy-start.3 = (bf16[128,512]{1,0:T(8,128)(2,1)S(1)}, bf16[128,512]{1,0:T(8,128)(2,1)}, u32[]{:S(2)}) copy-start(bf16[128,512]{1,0:T(8,128)(2,1)} %kg_ref.1) | copy-start | bytes 393220

commit v2 on v1

--- a/solution.py
+++ b/solution.py
@@ -19,9 +19,9 @@
 
 def kernel(
     n_isl, a, b,
-    x_ref, kg_ref, w_ref, g_ref, m_ref, gm_ref,
+    x_hbm, kg_hbm, w_hbm, g_ref, m_hbm, gm_ref,
     keys_ref, ig_ref, nw_ref, nm_ref, ng_ref, ngm_ref,
-    gw, xs, xr, kr, gs, gr, ge, dx, kacc,
+    x_ref, kg_ref, w_ref, m_ref, gw, xs, xr, kr, gs, gr, ge, dx, kacc, load,
     z_s, z_r, y_s, y_r, x_s, x_r, c_s, c_r, t_s, t_r, k_s, k_r, g_s, g_r, e_s, e_r,
 ):
     nq = 2 * b
@@ -50,6 +50,14 @@
     ys_ = [lax.rem(y + k, b) for k in range(b)]
     is_ = [lax.rem(isl + k, n_isl) for k in range(n_isl)]
 
+    loads = [
+        pltpu.make_async_copy(src, dst, load.at[i])
+        for i, (src, dst) in enumerate(
+            ((w_hbm, w_ref), (kg_hbm, kg_ref), (x_hbm, x_ref), (m_hbm, m_ref))
+        )
+    ]
+    for copy in loads:
+        copy.start()
     barrier = pltpu.get_barrier_semaphore()
     for k in range(1, a):
         pl.semaphore_signal(barrier, inc=1, device_id=dev(isl, zs_[k], q), device_id_type=MESH)
@@ -68,6 +76,7 @@
         ],
         axis=0,
     )
+    loads[0].wait()
     w_b = w_ref[...].astype(BF16).astype(F32)
     gw[z, q] = (w_b * gain_col).astype(BF16).reshape(2, rows // 2, feats)
     pl.semaphore_wait(barrier, a - 1 + nq - 1 + n_isl - 1)
@@ -119,10 +128,12 @@
 
     for k in range(1, a):
         go(z_copy(k))
+    loads[1].wait()
 
     for k in range(1, nq):
         go(remote(kg_ref, kr.at[q], k_s.at[k], k_r.at[k], dev(isl, z, qs_[k])))
 
+    loads[2].wait()
     acc = jnp.zeros((tokens, rows), F32)
     for p in range(n):
         xc = x_ref[:, p * rows : (p + 1) * rows].astype(F32)
@@ -131,8 +142,15 @@
     for p in range(n):
         xc = x_ref[:, p * rows : (p + 1) * rows].astype(F32)
         xs[p % nq, p // nq] = (xc * r).astype(BF16)
-    for k in range(1, nq):
-        go(remote(xs.at[qs_[k]], xr.at[q], t_s.at[k], t_r.at[k], dev(isl, z, qs_[k])))
+    near = list(range(1, a)) + [0]
+    for j in near:
+        for k in range(1, nq):
+            go(
+                remote(
+                    xs.at[qs_[k], zs_[j]], xr.at[q, zs_[j]],
+                    t_s.at[j, k], t_r.at[j, k], dev(isl, z, qs_[k]),
+                )
+            )
     xr[q] = xs[q]
     kr[q] = kg_ref[...]
 
@@ -151,9 +169,14 @@
     for k in range(1, nq):
         src = lax.rem(q + nq - k, nq)
         remote(kg_ref, kr.at[src], k_s.at[k], k_r.at[k], dev(isl, z, q)).wait_recv()
-        remote(xs.at[q], xr.at[src], t_s.at[k], t_r.at[k], dev(isl, z, q)).wait_recv()
-
-    def partial(zz):
+
+    def partial(j):
+        zz = zs_[j]
+        for k in range(1, nq):
+            src = lax.rem(q + nq - k, nq)
+            remote(
+                xs.at[q, zz], xr.at[src, zz], t_s.at[j, k], t_r.at[j, k], dev(isl, z, q)
+            ).wait_recv()
         return lax.dot_general(
             xr[:, zz].reshape(nq * tokens, rows),
             kr[...].reshape(nq * tokens, feats),
@@ -162,9 +185,9 @@
         )
 
     for k in range(1, a):
-        gs[k] = partial(zs_[k]).astype(BF16)
+        gs[k] = partial(k).astype(BF16)
         go(remote(gs.at[k], gr.at[k], g_s.at[k], g_r.at[k], dev(isl, zs_[k], q)))
-    own = partial(z)
+    own = partial(0)
 
     for zk in range(a):
         for k in range(1, b):
@@ -220,6 +243,7 @@
     total = total * (scale / n_isl)
     delta = total * gain_col * inner_rate
     w = w_ref[...]
+    loads[3].wait()
     fresh = beta_momentum * m_ref[...] + delta
     nm_ref[...] = fresh
     nw_ref[...] = w - outer_rate * (delta + beta_momentum * fresh)
@@ -235,6 +259,16 @@
         copy.wait_send()
 
 
+def store(*refs):
+    k = (len(refs) - 1) // 2
+    sem = refs[-1]
+    copies = [pltpu.make_async_copy(refs[i], refs[k + i], sem.at[i]) for i in range(k)]
+    for copy in copies:
+        copy.start()
+    for copy in copies:
+        copy.wait()
+
+
 def solution(mesh):
     n_isl, n = mesh.shape["island"], mesh.shape["fsdp"]
     b = 1
@@ -249,19 +283,25 @@
         sd = jax.ShapeDtypeStruct
         dma = pltpu.SemaphoreType.DMA
         vm = pl.BlockSpec(memory_space=pltpu.VMEM)
+        hbm = pl.BlockSpec(memory_space=pltpu.HBM)
+        shapes = (
+            sd((tokens, feats), BF16),
+            sd((tokens, width), BF16),
+            sd((rows, feats), F32),
+            sd((rows, feats), F32),
+            sd((1, rows), F32),
+            sd((1, rows), F32),
+        )
         outs = pl.pallas_call(
             functools.partial(kernel, n_isl, a, b),
-            out_shape=(
-                sd((tokens, feats), BF16),
-                sd((tokens, width), BF16),
-                sd((rows, feats), F32),
-                sd((rows, feats), F32),
-                sd((1, rows), F32),
-                sd((1, rows), F32),
-            ),
-            in_specs=[vm] * 6,
+            out_shape=shapes,
+            in_specs=[hbm, hbm, hbm, vm, hbm, vm],
             out_specs=[vm] * 6,
             scratch_shapes=[
+                pltpu.VMEM((tokens, width), BF16),
+                pltpu.VMEM((tokens, feats), BF16),
+                pltpu.VMEM((rows, feats), F32),
+                pltpu.VMEM((rows, feats), F32),
                 pltpu.VMEM((a, nq, 2, rows // 2, feats), BF16),
                 pltpu.VMEM((nq, a, tokens, rows), BF16),
                 pltpu.VMEM((nq, a, tokens, rows), BF16),
@@ -271,11 +311,12 @@
                 pltpu.VMEM((n_isl, rows, feats), BF16),
                 pltpu.VMEM((nq, a, tokens, rows), F32),
                 pltpu.VMEM((tokens, feats), F32),
+                dma((4,)),
                 dma((a,)), dma((a,)),
                 dma((a, b)), dma((a, b)),
                 dma((a, b)), dma((a, b)),
                 dma((a, b, 2)), dma((a, b, 2)),
-                dma((nq,)), dma((nq,)),
+                dma((a, nq)), dma((a, nq)),
                 dma((nq,)), dma((nq,)),
                 dma((a,)), dma((a,)),
                 dma((n_isl,)), dma((n_isl,)),
@@ -284,7 +325,13 @@
                 collective_id=0, has_side_effects=True, vmem_limit_bytes=48 << 20
             ),
         )(inputs, key_grad, weight, gain.reshape(1, rows), momentum, gain_momentum.reshape(1, rows))
-        keys, ig, nw, nm, ng, ngm = outs
+        keys, ig, nw, nm, ng, ngm = pl.pallas_call(
+            store,
+            out_shape=shapes,
+            in_specs=[vm] * 6,
+            out_specs=[hbm] * 6,
+            scratch_shapes=[dma((6,))],
+        )(*outs)
         return keys, ig, nw, nm, ng.reshape(rows), ngm.reshape(rows)
 
     in_specs = (

time: 61.4 us -> 62.6 us (1.020)
  Pallas kernels: 51.2 us -> 52.9 us
    pallas_call x1 -> x2, Pallas kernels: 51.2 us -> 52.9 us  [the longest x1 49.9 us: shards(): pl.pallas_call(functools.partial(kernel, n_isl, a, b), out_shape=shapes,...]
    unnamed x18 -> x24, local copies, waits for them, and re-layouts: 9.23 us -> 8.7 us
where the time goes in v2:
time: 62.6 us; the launch traced here: 62.2 us
  Pallas kernels  52.9 us (85%)
  local copies, waits for them, and re-layouts  8.7 us (14%)
  between operations  0.68 us (1%)
    pallas_call x1, Pallas kernels, shards(): pl.pallas_call(functools.partial(kernel, n_isl, a, b), out_shape=shapes,...  49.9 us
    unnamed x24, local copies, waits for them, and re-layouts  8.7 us
    pallas_call x1, Pallas kernels, shards(): pl.pallas_call(store, out_shape=shapes, in_specs=[vm] * 6, out_specs=[hbm...  2.97 us

profile of v2, /device:TPU:8, one launch (start us, length us, event | category | flops | bytes accessed | tf_op | source)
XLA Modules:
  0.0 62.2 jit_solution(5103457380052789322)
XLA Ops:
  0.6 0.0 copy-start.9
  0.6 0.0 copy-start.8
  0.7 0.7 %copy-done.9 = f32[256]{0:T(256)S(1)} copy-done((f32[256]{0:T(256)S(1)}, f32[256]{0:T(256)}, u32[]{:S(2)}) %copy-start.9) | copy-done | bytes 1048
  1.3 0.0 copy-done.8
  1.3 0.0 copy-start
  1.3 1.2 %copy-done = bf16[128,4096]{1,0:T(8,128)(2,1)S(1)} copy-done((bf16[128,4096]{1,0:T(8,128)(2,1)S(1)}, bf16[128,4096]{1,0:T(8,128)(2,1)}, u32[]{:S(2)}) %copy-start) | copy-done | bytes 1048600
  2.6 0.0 copy-start.2
  2.6 1.0 %copy-done.2 = f32[256,512]{1,0:T(8,128)S(1)} copy-done((f32[256,512]{1,0:T(8,128)S(1)}, f32[256,512]{1,0:T(8,128)}, u32[]{:S(2)}) %copy-start.2) | copy-done | bytes 524312
  3.6 0.0 copy-start.3
  3.6 1.0 %copy-done.3 = f32[256,512]{1,0:T(8,128)S(1)} copy-done((f32[256,512]{1,0:T(8,128)S(1)}, f32[256,512]{1,0:T(8,128)}, u32[]{:S(2)}) %copy-start.3) | copy-done | bytes 524312
  4.6 0.0 copy-start.6
  4.6 0.9 %copy-done.6 = bf16[128,512]{1,0:T(8,128)(2,1)S(1)} copy-done((bf16[128,512]{1,0:T(8,128)(2,1)S(1)}, bf16[128,512]{1,0:T(8,128)(2,1)}, u32[]{:S(2)}) %copy-start.6) | copy-done | bytes 131096
  5.5 49.9 %shard_map.109 = (bf16[128,512]{1,0:T(8,128)(2,1)S(1)}, bf16[128,4096]{1,0:T(8,128)(2,1)S(1)}, f32[256,512]{1,0:T(8,128)S(1)}, f32[256,512]{1,0:T(8,128)S(1)}, f...) custom-call(bf16[128,4096]{1,0:T(8,128)(2,1)S(1)} %copy-done, bf16[128,512]{1,0:T(8,128)(2,1)S(1)} %copy-done.6, ...), custom_call_target="tpu_custom_call" | custom-call | tf_op jit(solution)/shard_map/pallas_call | solution.py:295
  55.4 0.0 copy-start.1
  55.5 1.0 %copy-done.1 = bf16[128,4096]{1,0:T(8,128)(2,1)} copy-done((bf16[128,4096]{1,0:T(8,128)(2,1)}, bf16[128,4096]{1,0:T(8,128)(2,1)S(1)}, u32[]{:S(2)}) %copy-start.1) | copy-done | bytes 1048600
  56.4 0.0 copy-start.4
  56.4 0.8 %copy-done.4 = f32[256,512]{1,0:T(8,128)} copy-done((f32[256,512]{1,0:T(8,128)}, f32[256,512]{1,0:T(8,128)S(1)}, u32[]{:S(2)}) %copy-start.4) | copy-done | bytes 524312
  57.2 0.0 copy-start.5
  57.2 0.8 %copy-done.5 = f32[256,512]{1,0:T(8,128)} copy-done((f32[256,512]{1,0:T(8,128)}, f32[256,512]{1,0:T(8,128)S(1)}, u32[]{:S(2)}) %copy-start.5) | copy-done | bytes 524312
  58.0 0.0 copy-start.7
  58.1 0.6 %copy-done.7 = bf16[128,512]{1,0:T(8,128)(2,1)} copy-done((bf16[128,512]{1,0:T(8,128)(2,1)}, bf16[128,512]{1,0:T(8,128)(2,1)S(1)}, u32[]{:S(2)}) %copy-start.7) | copy-done | bytes 131096
  58.7 0.0 copy-start.10
  58.7 0.0 copy-start.11
  58.7 0.6 copy-done.10
  59.3 0.0 copy-done.11
  59.3 3.0 %shard_map.110 = (bf16[128,512]{1,0:T(8,128)(2,1)}, bf16[128,4096]{1,0:T(8,128)(2,1)}, f32[256,512]{1,0:T(8,128)}, f32[256,512]{1,0:T(8,128)}, f32[1,256]{1,0:T(1,128)}, /*index=5*/f32[1,256]{1,0:T(1,128)}) custom-call(bf16[128,512]{1,0:T(8,128)(2,1)} %copy-done.7, bf16[128,4096]{1,0:T(8,128)(2,1)} %copy-done.1, f32[256,512]{1,0:T(8,128)} %copy-done.4, ...), custom_call_target="tpu_custom_call" | custom-call | tf_op jit(solution)/shard_map/pallas_call | solution.py:328
Async XLA Ops:
  0.6 0.7 %copy-start.9 = (f32[256]{0:T(256)S(1)}, f32[256]{0:T(256)}, u32[]{:S(2)}) copy-start(f32[256]{0:T(256)} %param.11) | copy-start | bytes 3076
  0.6 0.7 %copy-start.8 = (f32[256]{0:T(256)S(1)}, f32[256]{0:T(256)}, u32[]{:S(2)}) copy-start(f32[256]{0:T(256)} %param.9) | copy-start | bytes 3076
  1.3 1.2 %copy-start = (bf16[128,4096]{1,0:T(8,128)(2,1)S(1)}, bf16[128,4096]{1,0:T(8,128)(2,1)}, u32[]{:S(2)}) copy-start(bf16[128,4096]{1,0:T(8,128)(2,1)} %x_hbm.1) | copy-start | bytes 3145732
  2.6 1.0 %copy-start.2 = (f32[256,512]{1,0:T(8,128)S(1)}, f32[256,512]{1,0:T(8,128)}, u32[]{:S(2)}) copy-start(f32[256,512]{1,0:T(8,128)} %w_hbm.1) | copy-start | bytes 1572868
  3.6 1.0 %copy-start.3 = (f32[256,512]{1,0:T(8,128)S(1)}, f32[256,512]{1,0:T(8,128)}, u32[]{:S(2)}) copy-start(f32[256,512]{1,0:T(8,128)} %m_hbm.1) | copy-start | bytes 1572868
  4.6 0.9 %copy-start.6 = (bf16[128,512]{1,0:T(8,128)(2,1)S(1)}, bf16[128,512]{1,0:T(8,128)(2,1)}, u32[]{:S(2)}) copy-start(bf16[128,512]{1,0:T(8,128)(2,1)} %kg_hbm.1) | copy-start | bytes 393220
  55.4 1.0 %copy-start.1 = (bf16[128,4096]{1,0:T(8,128)(2,1)}, bf16[128,4096]{1,0:T(8,128)(2,1)S(1)}, u32[]{:S(2)}) copy-start(bf16[128,4096]{1,0:T(8,128)(2,1)S(1)} %get-tuple-element.19.refs_1_) | copy-start | bytes 3145732
  56.4 0.8 %copy-start.4 = (f32[256,512]{1,0:T(8,128)}, f32[256,512]{1,0:T(8,128)S(1)}, u32[]{:S(2)}) copy-start(f32[256,512]{1,0:T(8,128)S(1)} %get-tuple-element.20.refs_2_) | copy-start | bytes 1572868
  57.2 0.8 %copy-start.5 = (f32[256,512]{1,0:T(8,128)}, f32[256,512]{1,0:T(8,128)S(1)}, u32[]{:S(2)}) copy-start(f32[256,512]{1,0:T(8,128)S(1)} %get-tuple-element.21.refs_3_) | copy-start | bytes 1572868
  58.0 0.6 %copy-start.7 = (bf16[128,512]{1,0:T(8,128)(2,1)}, bf16[128,512]{1,0:T(8,128)(2,1)S(1)}, u32[]{:S(2)}) copy-start(bf16[128,512]{1,0:T(8,128)(2,1)S(1)} %get-tuple-element.18.refs_0_) | copy-start | bytes 393220
  58.7 0.6 copy-start.10
  58.7 0.6 copy-start.11

commit v3 on v2

--- a/solution.py
+++ b/solution.py
@@ -19,9 +19,9 @@
 
 def kernel(
     n_isl, a, b,
-    x_hbm, kg_hbm, w_hbm, g_ref, m_hbm, gm_ref,
+    x_hbm, kg_hbm, w_hbm, g_hbm, m_hbm, gm_hbm,
     keys_ref, ig_ref, nw_ref, nm_ref, ng_ref, ngm_ref,
-    x_ref, kg_ref, w_ref, m_ref, gw, xs, xr, kr, gs, gr, ge, dx, kacc, load,
+    x_ref, kg_ref, w_ref, g_ref, m_ref, gm_ref, gw, xs, xr, kr, gs, gr, ge, dx, kacc, load,
     z_s, z_r, y_s, y_r, x_s, x_r, c_s, c_r, t_s, t_r, k_s, k_r, g_s, g_r, e_s, e_r,
 ):
     nq = 2 * b
@@ -53,7 +53,8 @@
     loads = [
         pltpu.make_async_copy(src, dst, load.at[i])
         for i, (src, dst) in enumerate(
-            ((w_hbm, w_ref), (kg_hbm, kg_ref), (x_hbm, x_ref), (m_hbm, m_ref))
+            ((w_hbm, w_ref), (kg_hbm, kg_ref), (x_hbm, x_ref), (m_hbm, m_ref),
+             (g_hbm, g_ref), (gm_hbm, gm_ref))
         )
     ]
     for copy in loads:
@@ -66,6 +67,8 @@
     for k in range(1, n_isl):
         pl.semaphore_signal(barrier, inc=1, device_id=dev(is_[k], z, q), device_id_type=MESH)
 
+    loads[4].wait()
+    loads[0].wait()
     lanes = min(rows, 128)
     gain_col = jnp.concatenate(
         [
@@ -76,7 +79,6 @@
         ],
         axis=0,
     )
-    loads[0].wait()
     w_b = w_ref[...].astype(BF16).astype(F32)
     gw[z, q] = (w_b * gain_col).astype(BF16).reshape(2, rows // 2, feats)
     pl.semaphore_wait(barrier, a - 1 + nq - 1 + n_isl - 1)
@@ -244,6 +246,7 @@
     delta = total * gain_col * inner_rate
     w = w_ref[...]
     loads[3].wait()
+    loads[5].wait()
     fresh = beta_momentum * m_ref[...] + delta
     nm_ref[...] = fresh
     nw_ref[...] = w - outer_rate * (delta + beta_momentum * fresh)
@@ -292,16 +295,19 @@
             sd((1, rows), F32),
             sd((1, rows), F32),
         )
+        stay = functools.partial(pltpu.with_memory_space_constraint, memory_space=pltpu.HBM)
         outs = pl.pallas_call(
             functools.partial(kernel, n_isl, a, b),
             out_shape=shapes,
-            in_specs=[hbm, hbm, hbm, vm, hbm, vm],
+            in_specs=[hbm] * 6,
             out_specs=[vm] * 6,
             scratch_shapes=[
                 pltpu.VMEM((tokens, width), BF16),
                 pltpu.VMEM((tokens, feats), BF16),
                 pltpu.VMEM((rows, feats), F32),
+                pltpu.VMEM((1, rows), F32),
                 pltpu.VMEM((rows, feats), F32),
+                pltpu.VMEM((1, rows), F32),
                 pltpu.VMEM((a, nq, 2, rows // 2, feats), BF16),
                 pltpu.VMEM((nq, a, tokens, rows), BF16),
                 pltpu.VMEM((nq, a, tokens, rows), BF16),
@@ -311,7 +317,7 @@
                 pltpu.VMEM((n_isl, rows, feats), BF16),
                 pltpu.VMEM((nq, a, tokens, rows), F32),
                 pltpu.VMEM((tokens, feats), F32),
-                dma((4,)),
+                dma((6,)),
                 dma((a,)), dma((a,)),
                 dma((a, b)), dma((a, b)),
                 dma((a, b)), dma((a, b)),
@@ -324,13 +330,17 @@
             compiler_params=pltpu.CompilerParams(
                 collective_id=0, has_side_effects=True, vmem_limit_bytes=48 << 20
             ),
-        )(inputs, key_grad, weight, gain.reshape(1, rows), momentum, gain_momentum.reshape(1, rows))
+        )(
+            stay(inputs), stay(key_grad), stay(weight), stay(gain.reshape(1, rows)),
+            stay(momentum), stay(gain_momentum.reshape(1, rows)),
+        )
         keys, ig, nw, nm, ng, ngm = pl.pallas_call(
             store,
             out_shape=shapes,
-            in_specs=[vm] * 6,
+            in_specs=[pl.BlockSpec(memory_space=pl.ANY)] * 6,
             out_specs=[hbm] * 6,
             scratch_shapes=[dma((6,))],
+            compiler_params=pltpu.CompilerParams(vmem_limit_bytes=1 << 20),
         )(*outs)
         return keys, ig, nw, nm, ng.reshape(rows), ngm.reshape(rows)
 

time: 62.6 us -> 51.9 us (0.83)
  local copies, waits for them, and re-layouts: 8.7 us -> 0 us
  Pallas kernels: 52.9 us -> 51.1 us
    unnamed x24 -> x0, local copies, waits for them, and re-layouts: 8.7 us -> none
    pallas_call x1, Pallas kernels: 2.97 us -> 1.41 us  [shards(): pl.pallas_call(store, out_shape=shapes, in_specs=[pl.BlockSpec(memory_spa...]
where the time goes in v3:
time: 51.9 us; the launch traced here: 51.7 us
  Pallas kernels  51.1 us (98%)
  between operations  0.64 us (1%)
    pallas_call x1, Pallas kernels, shards(): pl.pallas_call(functools.partial(kernel, n_isl, a, b), out_shape=shapes,...  49.7 us
    pallas_call x1, Pallas kernels, shards(): pl.pallas_call(store, out_shape=shapes, in_specs=[pl.BlockSpec(memory_spa...  1.41 us

profile of v3, /device:TPU:8, one launch (start us, length us, event | category | flops | bytes accessed | tf_op | source)
XLA Modules:
  0.0 51.7 jit_solution(12969303523504127308)
XLA Ops:
  0.6 49.7 %shard_map.109 = (bf16[128,512]{1,0:T(8,128)(2,1)S(1)}, bf16[128,4096]{1,0:T(8,128)(2,1)S(1)}, f32[256,512]{1,0:T(8,128)S(1)}, f32[256,512]{1,0:T(8,128)S(1)}, f...) custom-call(bf16[128,4096]{1,0:T(8,128)(2,1)} %x_hbm.1, bf16[128,512]{1,0:T(8,128)(2,1)} %kg_hbm.1, f32[256,512]{1,0:T(8,128)} %w_hbm.1, ...), custom_call_target="tpu_custom_call" | custom-call | tf_op jit(solution)/shard_map/pallas_call | solution.py:299
  50.3 1.4 %shard_map.110 = (bf16[128,512]{1,0:T(8,128)(2,1)}, bf16[128,4096]{1,0:T(8,128)(2,1)}, f32[256,512]{1,0:T(8,128)}, f32[256,512]{1,0:T(8,128)}, f32[1,256]{1,0:T(1,128)}, /*index=5*/f32[1,256]{1,0:T(1,128)}) custom-call(bf16[128,512]{1,0:T(8,128)(2,1)S(1)} %get-tuple-element.18.refs_0_, bf16[128,4096]{1,0:T(8,128)(2,1)S(1)} %get-tuple-element.19.refs_1_, ...), custom_call_target="tpu_custom_call" | custom-call | tf_op jit(solution)/shard_map/pallas_call | solution.py:337

commit v4 on v3

--- a/solution.py
+++ b/solution.py
@@ -134,6 +134,11 @@
 
     for k in range(1, nq):
         go(remote(kg_ref, kr.at[q], k_s.at[k], k_r.at[k], dev(isl, z, qs_[k])))
+
+    for k in range(1, b):
+        go(y_copy(0, k))
+    for h in range(2):
+        go(c_copy(0, 0, h))
 
     loads[2].wait()
     acc = jnp.zeros((tokens, rows), F32)
@@ -156,17 +161,17 @@
     xr[q] = xs[q]
     kr[q] = kg_ref[...]
 
-    for k in range(1, b):
-        go(y_copy(0, k))
-    for h in range(2):
-        go(c_copy(0, 0, h))
-
     for zk in range(1, a):
         z_wait(zk)
         for k in range(1, b):
             go(y_copy(zk, k))
         go(x_copy(zk, 0))
         go(c_copy(zk, 0, 0))
+
+    for k in range(1, b):
+        y_wait(0, k)
+        go(x_copy(0, k))
+        go(c_copy(0, k, 0))
 
     for k in range(1, nq):
         src = lax.rem(q + nq - k, nq)
@@ -191,7 +196,7 @@
         go(remote(gs.at[k], gr.at[k], g_s.at[k], g_r.at[k], dev(isl, zs_[k], q)))
     own = partial(0)
 
-    for zk in range(a):
+    for zk in range(1, a):
         for k in range(1, b):
             y_wait(zk, k)
             go(x_copy(zk, k))

time: 51.9 us -> 53.6 us (1.033)
  Pallas kernels: 51.1 us -> 52.8 us
    pallas_call x1, Pallas kernels: 49.7 us -> 51.4 us  [shards(): pl.pallas_call(functools.partial(kernel, n_isl, a, b), out_shape=shapes,...]
where the time goes in v4:
time: 53.6 us; the launch traced here: 53.5 us
  Pallas kernels  52.8 us (99%)
  between operations  0.64 us (1%)
    pallas_call x1, Pallas kernels, shards(): pl.pallas_call(functools.partial(kernel, n_isl, a, b), out_shape=shapes,...  51.4 us
    pallas_call x1, Pallas kernels, shards(): pl.pallas_call(store, out_shape=shapes, in_specs=[pl.BlockSpec(memory_spa...  1.41 us

profile of v4, /device:TPU:8, one launch (start us, length us, event | category | flops | bytes accessed | tf_op | source)
XLA Modules:
  0.0 53.5 jit_solution(7021834549210082052)
XLA Ops:
  0.6 51.4 %shard_map.109 = (bf16[128,512]{1,0:T(8,128)(2,1)S(1)}, bf16[128,4096]{1,0:T(8,128)(2,1)S(1)}, f32[256,512]{1,0:T(8,128)S(1)}, f32[256,512]{1,0:T(8,128)S(1)}, f...) custom-call(bf16[128,4096]{1,0:T(8,128)(2,1)} %x_hbm.1, bf16[128,512]{1,0:T(8,128)(2,1)} %kg_hbm.1, f32[256,512]{1,0:T(8,128)} %w_hbm.1, ...), custom_call_target="tpu_custom_call" | custom-call | tf_op jit(solution)/shard_map/pallas_call | solution.py:304
  52.0 1.4 %shard_map.110 = (bf16[128,512]{1,0:T(8,128)(2,1)}, bf16[128,4096]{1,0:T(8,128)(2,1)}, f32[256,512]{1,0:T(8,128)}, f32[256,512]{1,0:T(8,128)}, f32[1,256]{1,0:T(1,128)}, /*index=5*/f32[1,256]{1,0:T(1,128)}) custom-call(bf16[128,512]{1,0:T(8,128)(2,1)S(1)} %get-tuple-element.18.refs_0_, bf16[128,4096]{1,0:T(8,128)(2,1)S(1)} %get-tuple-element.19.refs_1_, ...), custom_call_target="tpu_custom_call" | custom-call | tf_op jit(solution)/shard_map/pallas_call | solution.py:342
